TPU v7x, 128 devices: a whole 4x4x4 slice. The times are simulated.
128 devices in a mesh: sa: 4 (over x), sb: 2 (over core), sc: 16 (over z, y).
Axes of the slice: x: 4, y: 4, z: 4, core: 2. Of those that a mesh axis runs over, the one named last changes fastest.
Arguments:
- queries: float32 [65536, 2048], P(('sa', 'sb', 'sc')), may hold values from -6 to 6
- key_rows: float32 [65536, 2048], P(('sa', 'sb', 'sc')), may hold values from -6 to 6
- value_rows: float32 [65536, 2048], P(('sa', 'sb', 'sc')), may hold values from -6 to 6
- out_grad: float32 [65536, 2048], P(('sa', 'sb', 'sc')), may hold values from -6 to 6
- prefix_state: float32 [16, 128, 128], replicated, may hold values from -1536 to 1536
- suffix_state: float32 [16, 128, 128], replicated, may hold values from -1536 to 1536
Outputs:
- query_grad: bfloat16 [65536, 2048], P(('sa', 'sb', 'sc'))
- key_grad: bfloat16 [65536, 2048], P(('sa', 'sb', 'sc'))
- value_grad: bfloat16 [65536, 2048], P(('sa', 'sb', 'sc'))
All inputs are finite; a program needn't handle non-finite values.
Results may differ from a plain program's by a relative error of at most 0.0019.
Values sent between devices are 32-bit elements; how exact they have to be, the bound alone decides.
A program may use at most 576 MiB of HBM per device.

v0:
```python
import math
import jax
import jax.numpy as jnp
from jax import lax
from jax.sharding import PartitionSpec as P


def entering(part, axis, combine, identity):
    place = lax.axis_index(axis)
    gathered = jax.tree.map(lambda a: lax.all_gather(a, axis), part)
    state = jax.tree.map(lambda a, e: jnp.zeros_like(a) + jnp.asarray(e, a.dtype), part, identity)

    def one(hop, state):
        return combine(
            state, jax.tree.map(lambda a: lax.dynamic_index_in_dim(a, hop, 0, False), gathered)
        )

    return lax.fori_loop(0, place, one, state)


def add_states(earlier, later):
    return jax.tree.map(lambda left, right: left + right, earlier, later)


def run_chain(local_terms):
    zero_state = jax.tree.map(jnp.zeros_like, local_terms)
    inner_part = entering(local_terms, "sc", add_states, zero_state)
    group_sum = lax.psum((local_terms[0], local_terms[1]), "sc")
    middle_part = entering(group_sum, "sb", add_states, zero_state)
    block_sum = lax.psum((group_sum[0], group_sum[1]), "sb")
    outer_part = entering(block_sum, "sa", add_states, zero_state)
    return add_states(add_states(outer_part, middle_part), inner_part)


def shards(queries, key_rows, value_rows, out_grad, prefix_state, suffix_state):
    row_count = queries.shape[0]
    head_count = prefix_state.shape[0]
    head_size = prefix_state.shape[1]
    device_count = lax.axis_size("sa") * lax.axis_size("sb") * lax.axis_size("sc")
    factor = 1.0 / math.sqrt(head_size * row_count * device_count)
    highest = lax.Precision.HIGHEST
    shaped = (row_count, head_count, head_size)
    query_t = queries.reshape(shaped)
    key_t = key_rows.reshape(shaped)
    value_t = value_rows.reshape(shaped)
    grad_t = out_grad.reshape(shaped)
    kv_local = jnp.einsum("thd,the->hde", key_t, value_t, precision=highest)
    grad_local = jnp.einsum("the,thd->hed", grad_t, query_t, precision=highest)
    prior_kv, prior_grad = run_chain((kv_local, grad_local))
    total_grad = lax.psum(grad_local, ("sa", "sb", "sc"))
    state_before = prefix_state + prior_kv
    state_after = suffix_state + (total_grad - prior_grad - grad_local)
    lower = (
        lax.broadcasted_iota(jnp.int32, (row_count, row_count), 0)
        >= lax.broadcasted_iota(jnp.int32, (row_count, row_count), 1)
    ).astype(jnp.float32)
    grad_scores = jnp.einsum("the,she->hts", grad_t, value_t, precision=highest) * lower
    attn_scores = jnp.einsum("thd,shd->hts", query_t, key_t, precision=highest) * lower
    query_grad = factor * (
        jnp.einsum("the,hde->thd", grad_t, state_before, precision=highest)
        + jnp.einsum("hts,shd->thd", grad_scores, key_t, precision=highest)
    )
    key_grad = factor * (
        jnp.einsum("she,hed->shd", value_t, state_after, precision=highest)
        + jnp.einsum("hts,thd->shd", grad_scores, query_t, precision=highest)
    )
    value_grad = factor * (
        jnp.einsum("shd,hed->she", key_t, state_after, precision=highest)
        + jnp.einsum("hts,the->she", attn_scores, grad_t, precision=highest)
    )
    flat = (row_count, head_count * head_size)
    return (
        query_grad.astype(jnp.bfloat16).reshape(flat),
        key_grad.astype(jnp.bfloat16).reshape(flat),
        value_grad.astype(jnp.bfloat16).reshape(flat),
    )


def solution(mesh):
    return jax.shard_map(
        shards,
        mesh=mesh,
        in_specs=(
            P(("sa", "sb", "sc"), None),
            P(("sa", "sb", "sc"), None),
            P(("sa", "sb", "sc"), None),
            P(("sa", "sb", "sc"), None),
            P(),
            P(),
        ),
        out_specs=(
            P(("sa", "sb", "sc"), None),
            P(("sa", "sb", "sc"), None),
            P(("sa", "sb", "sc"), None),
        ),
        check_vma=False,
    )
```

profile of v0, /device:TPU:1, one launch (start us, length us, event | category | flops | bytes accessed | tf_op | source)
XLA Modules:
  0.0 613.8 jit_solution(8954921210702635121)
XLA Ops:
  8.0 11.2 %fusion.21 = f32[16,128,128]{2,1,0:T(8,128)} fusion(f32[512,2048]{1,0:T(8,128)} %param.14, f32[512,2048]{1,0:T(8,128)} %param.13), kind=kOutput, calls=%fused_computation.27 | convolution fusion | flops 1610612736 | bytes 9437184 | tf_op jit(solution)/shard_map/thd,the->hde/dot_general | solution.py:47
  19.2 5.1 copy.46
  24.3 5.7 copy.27
  30.1 9.2 %fusion.16 = f32[16,128,128]{2,1,0:T(8,128)} fusion(f32[512,16,128]{0,2,1:T(8,128)} %copy.27, f32[512,2048]{1,0:T(8,128)} %param.12), kind=kOutput, calls=%fused_computation.22 | convolution fusion | flops 1610612736 | bytes 9437184 | tf_op jit(solution)/shard_map/the,thd->hed/dot_general | solution.py:48
  39.3 94.8 %all-gather.19.cloned.1.call-done = f32[256,128,128]{2,1,0:T(8,128)} async-done(((f32[16,128,128]{2,1,0:T(8,128)}), f32[256,128,128]{2,1,0:T(8,128)}) %all-gather.19.cloned.1.call-update) | async-done | bytes 16777232 | tf_op jit(solution)/shard_map/all_gather | solution.py:10
  134.0 0.7 all-reduce.8.cloned.1.call-update
  134.8 93.1 %all-reduce.8.cloned.1.call-done = (f32[16,128,128]{2,1,0:T(8,128)}, f32[16,128,128]{2,1,0:T(8,128)}) async-done(((f32[16,128,128]{2,1,0:T(8,128)}, f32[16,128,128]{2,1,0:T(8,128)}), (f32[16,128,128]{2,1,0:T(8,128)}, f32[16,128,128]{2,1,0:T(8,128)})) %all-reduce.8.cloned.1.call-update) | async-done | bytes 2097168 | tf_op jit(solution)/shard_map/psum | solution.py:28
  228.5 15.4 %all-gather.15.cloned.1.call-done = f32[32,128,128]{2,1,0:T(8,128)} async-done(((f32[16,128,128]{2,1,0:T(8,128)}), f32[32,128,128]{2,1,0:T(8,128)}) %all-gather.15.cloned.1.call-update) | async-done | bytes 2097168 | tf_op jit(solution)/shard_map/all_gather | solution.py:10
  243.9 16.3 %all-gather.17.cloned.1.call-done = f32[32,128,128]{2,1,0:T(8,128)} async-done(((f32[16,128,128]{2,1,0:T(8,128)}), f32[32,128,128]{2,1,0:T(8,128)}) %all-gather.17.cloned.1.call-update) | async-done | bytes 2097168 | tf_op jit(solution)/shard_map/all_gather | solution.py:10
  261.4 30.2 %all-reduce.10.cloned.1.call-done = (f32[1,16,128,128]{3,2,1,0:T(8,128)}, f32[1,16,128,128]{3,2,1,0:T(8,128)}) async-done(((f32[1,16,128,128]{3,2,1,0:T(8,128)}, f32[1,16,128,128]{3,2,1,0:T(8,128)}), (f32[1,16,128,128]{3,2,1,0:T(8,128)}, f32[1,16,128,128]{3,2,1,0:T(8,128)})) %all-reduce.10.cloned.1.call-update) | async-done | bytes 2097168 | tf_op jit(solution)/shard_map/psum | solution.py:30
  291.6 0.7 all-gather.13.cloned.1.call-update
  293.1 19.5 %fusion.14 = f32[16,512,512]{2,1,0:T(8,128)} fusion(f32[512,2048]{1,0:T(8,128)} %param.12, f32[512,2048]{1,0:T(8,128)} %param.13), kind=kOutput, calls=%fused_computation.20 | convolution fusion | flops 6442450944 | bytes 25165824 | tf_op jit(solution)/shard_map/thd,shd->hts/dot_general | solution.py:58
  312.6 14.5 %fusion.11 = f32[16,512,512]{2,1,0:T(8,128)S(1)} fusion(f32[512,2048]{1,0:T(8,128)S(1)} %copy-done.4, f32[512,2048]{1,0:T(8,128)S(1)} %copy-done.5), kind=kOutput, calls=%fused_computation.17 | convolution fusion | flops 6442450944 | bytes 25165824 | tf_op jit(solution)/shard_map/the,she->hts/dot_general | solution.py:57
  327.1 14.5 %fusion.2 = f32[16,512,128]{1,2,0:T(8,128)} fusion(f32[16,512,512]{2,1,0:T(8,128)S(1)} %fusion.11, f32[512,512]{1,0:T(8,128)S(1)} %fusion.55, f32[512,2048]{1,0:T(8,128)} %param.12), kind=kOutput, calls=%fused_computation.8 | convolution fusion | flops 6446645248 | bytes 26214400 | tf_op jit(solution)/shard_map/hts,thd->shd/dot_general | solution.py:65
  341.6 21.3 %fusion.4 = f32[16,512,128]{1,2,0:T(8,128)} fusion(f32[16,512,512]{2,1,0:T(8,128)S(1)} %fusion.11, f32[512,512]{1,0:T(8,128)S(1)} %fusion.55, f32[512,2048]{1,0:T(8,128)} %param.13), kind=kOutput, calls=%fused_computation.10 | convolution fusion | flops 6446645248 | bytes 26214400 | tf_op jit(solution)/shard_map/hts,shd->thd/dot_general | solution.py:61
  362.9 44.5 %all-gather.21.cloned.1.call-done = f32[256,128,128]{2,1,0:T(8,128)} async-done(((f32[16,128,128]{2,1,0:T(8,128)}), f32[256,128,128]{2,1,0:T(8,128)}) %all-gather.21.cloned.1.call-update) | async-done | bytes 16777232 | tf_op jit(solution)/shard_map/all_gather | solution.py:10
  407.6 1.0 copy-done.1
  408.8 2.1 while.37
  408.8 2.1 bitcast_add_fusion.13
  410.9 45.8 %all-gather.11.cloned.1.call-done = f32[4,16,128,128]{3,2,1,0:T(8,128)} async-done(((f32[1,16,128,128]{3,2,1,0:T(8,128)}), f32[4,16,128,128]{3,2,1,0:T(8,128)}) %all-gather.11.cloned.1.call-update) | async-done | bytes 4194320 | tf_op jit(solution)/shard_map/all_gather | solution.py:10
  456.7 50.5 %all-gather.13.cloned.1.call-done = f32[4,16,128,128]{3,2,1,0:T(8,128)} async-done(((f32[1,16,128,128]{3,2,1,0:T(8,128)}), f32[4,16,128,128]{3,2,1,0:T(8,128)}) %all-gather.13.cloned.1.call-update) | async-done | bytes 4194320 | tf_op jit(solution)/shard_map/all_gather | solution.py:10
  507.3 1.1 broadcast.6.clone.3
  508.4 44.6 %all-reduce.6.cloned.1.call-done = f32[16,128,128]{2,1,0:T(8,128)} async-done(((f32[16,128,128]{2,1,0:T(8,128)}), f32[16,128,128]{2,1,0:T(8,128)}) %all-reduce.6.cloned.1.call-update) | async-done | bytes 1048592 | tf_op jit(solution)/shard_map/psum | solution.py:50
  552.9 3.5 subtract_add_fusion
  556.4 1.0 copy-done.8
  557.5 3.8 fusion.23
  561.3 14.6 %fusion.29 = bf16[512,16,128]{0,2,1:T(8,128)(2,1)} fusion(f32[16,128,512]{2,1,0:T(8,128)S(1)} %fusion.23, f32[512,16,128]{0,2,1:T(8,128)S(1)} %copy-done.3, f32[16,512,512]{2,1,0:T(8,128)} %fusion.14, f32[512,512]{1,0:T(8,128)S(1)} %copy-done.7), kind=kOutput, calls=%fused_computation.36 | convolution fusion | flops 6449790976 | bytes 28311552 | tf_op jit(solution)/shard_map/hts,the->she/dot_general | solution.py:69
  575.9 3.9 copy.40
  579.8 9.2 %fusion.31 = bf16[512,16,128]{0,2,1:T(8,128)(2,1)} fusion(f32[16,512,128]{1,2,0:T(8,128)} %fusion.2, f32[16,128,128]{2,1,0:T(8,128)} %copy-done.8, f32[512,2048]{1,0:T(8,128)} %param.14), kind=kOutput, calls=%fused_computation.39 | convolution fusion | flops 1613758464 | bytes 11534336 | tf_op jit(solution)/shard_map/she,hed->shd/dot_general | solution.py:64
  589.0 4.1 copy.39
  593.1 9.2 %fusion.33 = bf16[512,16,128]{0,2,1:T(8,128)(2,1)} fusion(f32[16,512,128]{1,2,0:T(8,128)} %fusion.4, f32[16,128,128]{2,1,0:T(8,128)} %param.16, f32[16,128,128]{2,1,0:T(8,128)S(1)} %get-tuple-element.107, f32[16,128,128]{2,1,0:T(8,128)S(1)} %get-tuple-element.105, f32[16,128,128]{2,1,0:T(8,128)S(1)} %get-tuple-element.106, f32[512,2048]{1,0:T(8,128)} %param.15), kind=kOutput, calls=%fused_computation.42 | convolution fusion | flops 1614544896 | bytes 14680064 | tf_op jit(solution)/shard_map/the,hde->thd/dot_general | solution.py:60
  602.3 3.9 copy.38
  (40 shorter events, 3.1 us)
Async XLA Ops:
  8.0 126.0 %all-gather.19.cloned.1.call-start = ((), (), s32[]{:S(2)}) async-start(), calls=%async_computation.5 | async-start | bytes 17825792 | tf_op jit(solution)/shard_map/all_gather | solution.py:10
  134.0 93.9 %all-reduce.8.cloned.1.call-start = ((), (), s32[]{:S(2)}) async-start(), calls=%async_computation.7 | async-start | bytes 4194304 | tf_op jit(solution)/shard_map/psum | solution.py:28
  134.8 109.2 %all-gather.15.cloned.1.call-start = ((), (), s32[]{:S(2)}) async-start(), calls=%async_computation.3 | async-start | bytes 3145728 | tf_op jit(solution)/shard_map/all_gather | solution.py:10
  228.0 32.2 %all-gather.17.cloned.1.call-start = ((), (), s32[]{:S(2)}) async-start(), calls=%async_computation.4 | async-start | bytes 3145728 | tf_op jit(solution)/shard_map/all_gather | solution.py:10
  260.2 31.4 %all-reduce.10.cloned.1.call-start = ((), (), s32[]{:S(2)}) async-start(), calls=%async_computation.8 | async-start | bytes 4194304 | tf_op jit(solution)/shard_map/psum | solution.py:30
  260.8 146.6 %all-gather.21.cloned.1.call-start = ((), (), s32[]{:S(2)}) async-start(), calls=%async_computation.6 | async-start | bytes 17825792 | tf_op jit(solution)/shard_map/all_gather | solution.py:10
  261.4 195.3 %all-gather.11.cloned.1.call-start = ((), (), s32[]{:S(2)}) async-start(), calls=%async_computation | async-start | bytes 5242880 | tf_op jit(solution)/shard_map/all_gather | solution.py:10
  291.6 215.6 %all-gather.13.cloned.1.call-start = ((), (), s32[]{:S(2)}) async-start(), calls=%async_computation.1 | async-start | bytes 5242880 | tf_op jit(solution)/shard_map/all_gather | solution.py:10
  292.3 260.6 %all-reduce.6.cloned.1.call-start = ((), (), s32[]{:S(2)}) async-start(), calls=%async_computation.2 | async-start | bytes 2097152 | tf_op jit(solution)/shard_map/psum | solution.py:50
  293.0 48.6 %copy-start.6 = (f32[512,512]{1,0:T(8,128)}, f32[512,512]{1,0:T(8,128)S(1)}, u32[]{:S(2)}) copy-start(f32[512,512]{1,0:T(8,128)S(1)} %fusion.55) | copy-start | bytes 3145732
  293.1 19.6 %copy-start.4 = (f32[512,2048]{1,0:T(8,128)S(1)}, f32[512,2048]{1,0:T(8,128)}, u32[]{:S(2)}) copy-start(f32[512,2048]{1,0:T(8,128)} %param.15) | copy-start | bytes 12582916
  293.1 19.6 %copy-start.5 = (f32[512,2048]{1,0:T(8,128)S(1)}, f32[512,2048]{1,0:T(8,128)}, u32[]{:S(2)}) copy-start(f32[512,2048]{1,0:T(8,128)} %param.14) | copy-start | bytes 12582916
  407.6 1.0 copy-start.1
  410.9 45.8 %copy-start.2 = (f32[16,128,128]{2,1,0:T(8,128)}, f32[16,128,128]{2,1,0:T(8,128)S(1)}, u32[]{:S(2)}) copy-start(f32[16,128,128]{2,1,0:T(8,128)S(1)} %get-tuple-element.109) | copy-start | bytes 3145732
  552.9 4.5 copy-start
  556.4 1.0 copy-start.8
  557.5 3.8 copy-start.3
  557.5 3.8 copy-start.7
Sparse Core Ops, SparseCore 0:
  19.4 114.6 all-gather.18
  138.8 89.0 all-reduce.7
  229.7 14.2 all-gather.14
  245.5 14.6 all-gather.16
  263.4 28.1 all-reduce.9
  294.1 113.1 all-gather.20
  409.0 47.6 all-gather.10
  458.3 48.7 all-gather.12
Sparse Core Ops, SparseCore 1:
  298.2 254.7 all-reduce.5
where the time goes:
time: 621 us; the launch traced here: 614 us
  waiting for transfers between devices  439 us (71%)
  matrix products  127 us (20%)
  local copies, waits for them, and re-layouts  26.3 us (4%)
  between operations  16 us (3%)
    all_gather x6, waiting for transfers between devices, entering(): gathered = jax.tree.map(lambda a: lax.all_gather(a, axis), part)  267 us
    psum x1, waiting for transfers between devices, run_chain(): group_sum = lax.psum((local_terms[0], local_terms[1]), 'sc')  93.1 us
    psum x1, waiting for transfers between devices, shards(): total_grad = lax.psum(grad_local, ('sa', 'sb', 'sc'))  44.6 us
    psum x1, waiting for transfers between devices, run_chain(): block_sum = lax.psum((group_sum[0], group_sum[1]), 'sb')  30.2 us
    dot_general x1, matrix products, shards(): jnp.einsum('hts,shd->thd', grad_scores, key_t, precision=highest)  21.3 us
    dot_general x1, matrix products, shards(): jnp.einsum('thd,shd->hts', query_t, key_t, precision=highest) * lower  19.5 us
    unnamed x22, local copies, waits for them, and re-layouts  19 us
    dot_general x1, matrix products, shards(): jnp.einsum('hts,the->she', attn_scores, grad_t, precision=highest)  14.6 us
  transfers between devices with their start and end apart: 9, of which 9 were waited for; matrix products, arithmetic and copies ran while one was open for 15% of the time, Pallas kernels for 0%

commit v1 on v0

--- a/solution.py
+++ b/solution.py
@@ -47,7 +47,7 @@
     kv_local = jnp.einsum("thd,the->hde", key_t, value_t, precision=highest)
     grad_local = jnp.einsum("the,thd->hed", grad_t, query_t, precision=highest)
     prior_kv, prior_grad = run_chain((kv_local, grad_local))
-    total_grad = lax.psum(grad_local, ("sa", "sb", "sc"))
+    total_grad = lax.psum(lax.psum(grad_local, ("sb", "sc")), "sa")
     state_before = prefix_state + prior_kv
     state_after = suffix_state + (total_grad - prior_grad - grad_local)
     lower = (

time: 621 us -> 729 us (1.17)
  waiting for transfers between devices: 439 us -> 548 us
    all_gather x6, waiting for transfers between devices: 267 us -> 337 us  [entering(): gathered = jax.tree.map(lambda a: lax.all_gather(a, axis), part)]
    psum x1 -> x2, waiting for transfers between devices: 44.6 us -> 84.7 us  [shards(): total_grad = lax.psum(lax.psum(grad_local, ('sb', 'sc')), 'sa')]
  transfers between devices with their start and end apart: 9 -> 10, of which waited for: 9 -> 10; matrix products, arithmetic and copies ran while one was open for 15% -> 13% of each run, Pallas kernels for 0% -> 0%
where the time goes in v1:
time: 729 us; the launch traced here: 722 us
  waiting for transfers between devices  548 us (75%)
  matrix products  127 us (17%)
  local copies, waits for them, and re-layouts  26.3 us (4%)
  between operations  14.6 us (2%)
    all_gather x6, waiting for transfers between devices, entering(): gathered = jax.tree.map(lambda a: lax.all_gather(a, axis), part)  337 us
    psum x1, waiting for transfers between devices, run_chain(): group_sum = lax.psum((local_terms[0], local_terms[1]), 'sc')  93.1 us
    psum x2, waiting for transfers between devices, shards(): total_grad = lax.psum(lax.psum(grad_local, ('sb', 'sc')), 'sa')  84.7 us
    psum x1, waiting for transfers between devices, run_chain(): block_sum = lax.psum((group_sum[0], group_sum[1]), 'sb')  29.4 us
    dot_general x1, matrix products, shards(): jnp.einsum('hts,shd->thd', grad_scores, key_t, precision=highest)  20.9 us
    dot_general x1, matrix products, shards(): jnp.einsum('thd,shd->hts', query_t, key_t, precision=highest) * lower  19.5 us
    unnamed x22, local copies, waits for them, and re-layouts  19 us
    dot_general x1, matrix products, shards(): jnp.einsum('hts,thd->shd', grad_scores, query_t, precision=highest)  14.8 us
  transfers between devices with their start and end apart: 10, of which 10 were waited for; matrix products, arithmetic and copies ran while one was open for 13% of the time, Pallas kernels for 0%

profile of v1, /device:TPU:1, one launch (start us, length us, event | category | flops | bytes accessed | tf_op | source)
XLA Modules:
  0.0 721.8 jit_solution(10570711667916914884)
XLA Ops:
  7.2 11.2 %fusion.21 = f32[16,128,128]{2,1,0:T(8,128)} fusion(f32[512,2048]{1,0:T(8,128)} %param.14, f32[512,2048]{1,0:T(8,128)} %param.13), kind=kOutput, calls=%fused_computation.27 | convolution fusion | flops 1610612736 | bytes 9437184 | tf_op jit(solution)/shard_map/thd,the->hde/dot_general | solution.py:47
  18.4 5.1 copy.46
  23.5 5.7 copy.27
  29.2 9.2 %fusion.16 = f32[16,128,128]{2,1,0:T(8,128)} fusion(f32[512,16,128]{0,2,1:T(8,128)} %copy.27, f32[512,2048]{1,0:T(8,128)} %param.12), kind=kOutput, calls=%fused_computation.22 | convolution fusion | flops 1610612736 | bytes 9437184 | tf_op jit(solution)/shard_map/the,thd->hed/dot_general | solution.py:48
  38.4 94.8 %all-gather.19.cloned.1.call-done = f32[256,128,128]{2,1,0:T(8,128)} async-done(((f32[16,128,128]{2,1,0:T(8,128)}), f32[256,128,128]{2,1,0:T(8,128)}) %all-gather.19.cloned.1.call-update) | async-done | bytes 16777232 | tf_op jit(solution)/shard_map/all_gather | solution.py:10
  133.2 0.7 all-reduce.11.cloned.1.call-update
  134.0 93.1 %all-reduce.11.cloned.1.call-done = (f32[16,128,128]{2,1,0:T(8,128)}, f32[16,128,128]{2,1,0:T(8,128)}) async-done(((f32[16,128,128]{2,1,0:T(8,128)}, f32[16,128,128]{2,1,0:T(8,128)}), (f32[16,128,128]{2,1,0:T(8,128)}, f32[16,128,128]{2,1,0:T(8,128)})) %all-reduce.11.cloned.1.call-update) | async-done | bytes 2097168 | tf_op jit(solution)/shard_map/psum | solution.py:28
  227.7 15.4 %all-gather.15.cloned.1.call-done = f32[32,128,128]{2,1,0:T(8,128)} async-done(((f32[16,128,128]{2,1,0:T(8,128)}), f32[32,128,128]{2,1,0:T(8,128)}) %all-gather.15.cloned.1.call-update) | async-done | bytes 2097168 | tf_op jit(solution)/shard_map/all_gather | solution.py:10
  243.1 16.3 %all-gather.17.cloned.1.call-done = f32[32,128,128]{2,1,0:T(8,128)} async-done(((f32[16,128,128]{2,1,0:T(8,128)}), f32[32,128,128]{2,1,0:T(8,128)}) %all-gather.17.cloned.1.call-update) | async-done | bytes 2097168 | tf_op jit(solution)/shard_map/all_gather | solution.py:10
  261.3 29.4 %all-reduce.13.cloned.1.call-done = (f32[1,16,128,128]{3,2,1,0:T(8,128)}, f32[1,16,128,128]{3,2,1,0:T(8,128)}) async-done(((f32[1,16,128,128]{3,2,1,0:T(8,128)}, f32[1,16,128,128]{3,2,1,0:T(8,128)}), (f32[1,16,128,128]{3,2,1,0:T(8,128)}, f32[1,16,128,128]{3,2,1,0:T(8,128)})) %all-reduce.13.cloned.1.call-update) | async-done | bytes 2097168 | tf_op jit(solution)/shard_map/psum | solution.py:30
  291.7 19.5 %fusion.14 = f32[16,512,512]{2,1,0:T(8,128)} fusion(f32[512,2048]{1,0:T(8,128)} %param.12, f32[512,2048]{1,0:T(8,128)} %param.13), kind=kOutput, calls=%fused_computation.20 | convolution fusion | flops 6442450944 | bytes 25165824 | tf_op jit(solution)/shard_map/thd,shd->hts/dot_general | solution.py:58
  311.3 14.5 %fusion.11 = f32[16,512,512]{2,1,0:T(8,128)S(1)} fusion(f32[512,2048]{1,0:T(8,128)S(1)} %copy-done.4, f32[512,2048]{1,0:T(8,128)S(1)} %copy-done.5), kind=kOutput, calls=%fused_computation.17 | convolution fusion | flops 6442450944 | bytes 25165824 | tf_op jit(solution)/shard_map/the,she->hts/dot_general | solution.py:57
  325.7 20.9 %fusion.4 = f32[16,512,128]{1,2,0:T(8,128)} fusion(f32[16,512,512]{2,1,0:T(8,128)S(1)} %fusion.11, f32[512,512]{1,0:T(8,128)S(1)} %fusion.55, f32[512,2048]{1,0:T(8,128)} %param.13), kind=kOutput, calls=%fused_computation.10 | convolution fusion | flops 6446645248 | bytes 26214400 | tf_op jit(solution)/shard_map/hts,shd->thd/dot_general | solution.py:61
  346.7 14.8 %fusion.2 = f32[16,512,128]{1,2,0:T(8,128)} fusion(f32[16,512,512]{2,1,0:T(8,128)S(1)} %fusion.11, f32[512,512]{1,0:T(8,128)S(1)} %fusion.55, f32[512,2048]{1,0:T(8,128)} %param.12), kind=kOutput, calls=%fused_computation.8 | convolution fusion | flops 6446645248 | bytes 26214400 | tf_op jit(solution)/shard_map/hts,thd->shd/dot_general | solution.py:65
  361.5 38.8 %all-reduce.7.cloned.1.call-done = f32[16,128,128]{2,1,0:T(8,128)} async-done(((f32[16,128,128]{2,1,0:T(8,128)}), f32[16,128,128]{2,1,0:T(8,128)}) %all-reduce.7.cloned.1.call-update) | async-done | bytes 1048592 | tf_op jit(solution)/shard_map/psum | solution.py:50
  400.3 114.1 %all-gather.21.cloned.1.call-done = f32[256,128,128]{2,1,0:T(8,128)} async-done(((f32[16,128,128]{2,1,0:T(8,128)}), f32[256,128,128]{2,1,0:T(8,128)}) %all-gather.21.cloned.1.call-update) | async-done | bytes 16777232 | tf_op jit(solution)/shard_map/all_gather | solution.py:10
  514.7 1.0 copy-done.1
  515.8 2.1 while.37
  515.9 2.1 bitcast_add_fusion.13
  518.0 46.1 %all-gather.11.cloned.1.call-done = f32[4,16,128,128]{3,2,1,0:T(8,128)} async-done(((f32[1,16,128,128]{3,2,1,0:T(8,128)}), f32[4,16,128,128]{3,2,1,0:T(8,128)}) %all-gather.11.cloned.1.call-update) | async-done | bytes 4194320 | tf_op jit(solution)/shard_map/all_gather | solution.py:10
  564.1 50.4 %all-gather.13.cloned.1.call-done = f32[4,16,128,128]{3,2,1,0:T(8,128)} async-done(((f32[1,16,128,128]{3,2,1,0:T(8,128)}), f32[4,16,128,128]{3,2,1,0:T(8,128)}) %all-gather.13.cloned.1.call-update) | async-done | bytes 4194320 | tf_op jit(solution)/shard_map/all_gather | solution.py:10
  614.6 1.1 broadcast.6.clone.3
  615.7 45.9 %all-reduce.9.cloned.1.call-done = f32[16,128,128]{2,1,0:T(8,128)} async-done(((f32[16,128,128]{2,1,0:T(8,128)}), f32[16,128,128]{2,1,0:T(8,128)}) %all-reduce.9.cloned.1.call-update) | async-done | bytes 1048592 | tf_op jit(solution)/shard_map/psum | solution.py:50
  661.6 3.5 subtract_add_fusion
  665.1 1.0 copy-done.8
  666.1 3.8 fusion.23
  669.9 14.6 %fusion.29 = bf16[512,16,128]{0,2,1:T(8,128)(2,1)} fusion(f32[16,128,512]{2,1,0:T(8,128)S(1)} %fusion.23, f32[512,16,128]{0,2,1:T(8,128)S(1)} %copy-done.3, f32[16,512,512]{2,1,0:T(8,128)} %fusion.14, f32[512,512]{1,0:T(8,128)S(1)} %copy-done.7), kind=kOutput, calls=%fused_computation.36 | convolution fusion | flops 6449790976 | bytes 28311552 | tf_op jit(solution)/shard_map/hts,the->she/dot_general | solution.py:69
  684.5 3.9 copy.40
  688.4 9.2 %fusion.31 = bf16[512,16,128]{0,2,1:T(8,128)(2,1)} fusion(f32[16,512,128]{1,2,0:T(8,128)} %fusion.2, f32[16,128,128]{2,1,0:T(8,128)} %copy-done.8, f32[512,2048]{1,0:T(8,128)} %param.14), kind=kOutput, calls=%fused_computation.39 | convolution fusion | flops 1613758464 | bytes 11534336 | tf_op jit(solution)/shard_map/she,hed->shd/dot_general | solution.py:64
  697.6 4.1 copy.39
  701.7 9.2 %fusion.33 = bf16[512,16,128]{0,2,1:T(8,128)(2,1)} fusion(f32[16,512,128]{1,2,0:T(8,128)} %fusion.4, f32[16,128,128]{2,1,0:T(8,128)} %param.16, f32[16,128,128]{2,1,0:T(8,128)S(1)} %get-tuple-element.107, f32[16,128,128]{2,1,0:T(8,128)S(1)} %get-tuple-element.105, f32[16,128,128]{2,1,0:T(8,128)S(1)} %get-tuple-element.106, f32[512,2048]{1,0:T(8,128)} %param.15), kind=kOutput, calls=%fused_computation.42 | convolution fusion | flops 1614544896 | bytes 14680064 | tf_op jit(solution)/shard_map/the,hde->thd/dot_general | solution.py:60
  710.9 3.9 copy.38
  (43 shorter events, 4.0 us)
Async XLA Ops:
  7.2 126.0 %all-gather.19.cloned.1.call-start = ((), (), s32[]{:S(2)}) async-start(), calls=%async_computation.6 | async-start | bytes 17825792 | tf_op jit(solution)/shard_map/all_gather | solution.py:10
  133.2 93.9 %all-reduce.11.cloned.1.call-start = ((), (), s32[]{:S(2)}) async-start(), calls=%async_computation.8 | async-start | bytes 4194304 | tf_op jit(solution)/shard_map/psum | solution.py:28
  133.9 109.2 %all-gather.15.cloned.1.call-start = ((), (), s32[]{:S(2)}) async-start(), calls=%async_computation.4 | async-start | bytes 3145728 | tf_op jit(solution)/shard_map/all_gather | solution.py:10
  227.1 32.2 %all-gather.17.cloned.1.call-start = ((), (), s32[]{:S(2)}) async-start(), calls=%async_computation.5 | async-start | bytes 3145728 | tf_op jit(solution)/shard_map/all_gather | solution.py:10
  259.4 31.4 %all-reduce.13.cloned.1.call-start = ((), (), s32[]{:S(2)}) async-start(), calls=%async_computation.9 | async-start | bytes 4194304 | tf_op jit(solution)/shard_map/psum | solution.py:30
  259.9 140.4 %all-reduce.7.cloned.1.call-start = ((), (), s32[]{:S(2)}) async-start(), calls=%async_computation.2 | async-start | bytes 2097152 | tf_op jit(solution)/shard_map/psum | solution.py:50
  260.5 253.9 %all-gather.21.cloned.1.call-start = ((), (), s32[]{:S(2)}) async-start(), calls=%async_computation.7 | async-start | bytes 17825792 | tf_op jit(solution)/shard_map/all_gather | solution.py:10
  261.3 302.8 %all-gather.11.cloned.1.call-start = ((), (), s32[]{:S(2)}) async-start(), calls=%async_computation | async-start | bytes 5242880 | tf_op jit(solution)/shard_map/all_gather | solution.py:10
  290.8 323.7 %all-gather.13.cloned.1.call-start = ((), (), s32[]{:S(2)}) async-start(), calls=%async_computation.1 | async-start | bytes 5242880 | tf_op jit(solution)/shard_map/all_gather | solution.py:10
  291.5 370.1 %all-reduce.9.cloned.1.call-start = ((), (), s32[]{:S(2)}) async-start(), calls=%async_computation.3 | async-start | bytes 2097152 | tf_op jit(solution)/shard_map/psum | solution.py:50
  291.7 55.0 %copy-start.6 = (f32[512,512]{1,0:T(8,128)}, f32[512,512]{1,0:T(8,128)S(1)}, u32[]{:S(2)}) copy-start(f32[512,512]{1,0:T(8,128)S(1)} %fusion.55) | copy-start | bytes 3145732
  291.7 19.6 %copy-start.4 = (f32[512,2048]{1,0:T(8,128)S(1)}, f32[512,2048]{1,0:T(8,128)}, u32[]{:S(2)}) copy-start(f32[512,2048]{1,0:T(8,128)} %param.15) | copy-start | bytes 12582916
  291.7 19.6 %copy-start.5 = (f32[512,2048]{1,0:T(8,128)S(1)}, f32[512,2048]{1,0:T(8,128)}, u32[]{:S(2)}) copy-start(f32[512,2048]{1,0:T(8,128)} %param.14) | copy-start | bytes 12582916
  514.7 1.0 copy-start.1
  518.0 46.1 %copy-start.2 = (f32[16,128,128]{2,1,0:T(8,128)}, f32[16,128,128]{2,1,0:T(8,128)S(1)}, u32[]{:S(2)}) copy-start(f32[16,128,128]{2,1,0:T(8,128)S(1)} %get-tuple-element.109) | copy-start | bytes 3145732
  661.5 4.5 copy-start
  665.1 1.0 copy-start.8
  666.1 3.8 copy-start.3
  666.1 3.8 copy-start.7
Sparse Core Ops, SparseCore 0:
  18.5 114.6 all-gather.18
  138.0 89.0 all-reduce.10
  228.9 14.2 all-gather.14
  244.7 14.6 all-gather.16
  262.5 28.1 all-reduce.12
  294.4 105.8 all-reduce.6
  403.2 111.1 all-gather.20
  516.2 47.8 all-gather.10
  565.9 48.5 all-gather.12
  616.8 44.7 all-reduce.8
